TPU v7x, 32 devices: a whole 2x2x4 slice. The times are simulated.
32 devices in a mesh: dp: 16 (over z, x, core), head: 2 (over y).
Axes of the slice: x: 2, y: 2, z: 4, core: 2. Of those that a mesh axis runs over, the one named last changes fastest.
Arguments:
- tokens: bfloat16 [16384, 1024], P(('dp', 'head')), may hold values from -6 to 6
- lengths: int32 [16], P('dp'), may hold values from 128 to 1024, as said below
- decay: float32 [8], P('head'), may hold values from 0.00048828125 to 0.03125
- w_query: bfloat16 [1024, 1024], P(None, 'head'), may hold values from -0.1875 to 0.1875
- w_key: bfloat16 [1024, 1024], P(None, 'head'), may hold values from -0.1875 to 0.1875
- w_value: bfloat16 [1024, 1024], P(None, 'head'), may hold values from -0.1875 to 0.1875
- w_gate: bfloat16 [1024, 1024], P(None, 'head'), may hold values from -0.1875 to 0.1875
- w_out: bfloat16 [1024, 1024], P('head'), may hold values from -0.1875 to 0.1875
- f_value: bfloat16 [1024, 2816], P('dp', 'head'), may hold values from -0.1875 to 0.1875
- f_gate: bfloat16 [1024, 2816], P('dp', 'head'), may hold values from -0.1875 to 0.1875
- f_out: bfloat16 [2816, 1024], P('head', 'dp'), may hold values from -0.109375 to 0.109375
- cotangent: bfloat16 [16384, 1024], P(('dp', 'head')), may hold values from -6 to 6
Outputs:
- output: bfloat16 [16384, 1024], P(('dp', 'head'))
- d_tokens: float32 [16384, 1024], P(('dp', 'head'))
- d_w_query: float32 [1024, 1024], P(None, 'head')
- d_w_key: float32 [1024, 1024], P(None, 'head')
- d_w_value: float32 [1024, 1024], P(None, 'head')
- d_w_gate: float32 [1024, 1024], P(None, 'head')
- d_w_out: float32 [1024, 1024], P('head')
- d_f_value: float32 [1024, 2816], P('dp', 'head')
- d_f_gate: float32 [1024, 2816], P('dp', 'head')
- d_f_out: float32 [2816, 1024], P('head', 'dp')
Inputs may be any that keep to these rules, and one draw needn't show every extreme that they name: `lengths`: each bucket holds a single slot, and that slot's sequence has length 1024.
All inputs are finite; a program needn't handle non-finite values.
Results may differ from a plain program's by a relative error of at most 0.022.
Values may be sent and summed in bfloat16 or wider, within the bound.
A program may use at most 192 MiB of HBM per device.

v0:
```python
import jax
import jax.numpy as jnp
from jax import lax
from jax.sharding import PartitionSpec as P

D = 1024
HD = 128
SEQ_DEV = 1
SLOT = 1024
BLOCK = 512
epsilon = 1e-06


def normalize(values):
    factor = lax.rsqrt(jnp.mean(values * values, axis=-1, keepdims=True) + epsilon)
    return (values * factor, factor)


def norm_back(grad_normed, normed, factor):
    inner_sum = jnp.mean(grad_normed * normed, axis=-1, keepdims=True)
    return factor * (grad_normed - normed * inner_sum)


def silu_slope(values):
    sigmoid = jax.nn.sigmoid(values)
    return sigmoid * (1.0 + values * (1.0 - sigmoid))


def matmul(left_side, right_side):
    return jnp.dot(left_side, right_side, preferred_element_type=jnp.float32)


def matmul_right_t(left_side, right_side):
    return lax.dot_general(
        left_side, right_side, (((1,), (1,)), ((), ())), preferred_element_type=jnp.float32
    )


def matmul_left_t(left_side, right_side):
    return lax.dot_general(
        left_side, right_side, (((0,), (0,)), ((), ())), preferred_element_type=jnp.float32
    )


def exact(form, left_side, right_side):
    return jnp.einsum(form, left_side, right_side, precision=lax.Precision.HIGHEST)


def decay_tables(rates):
    offsets = jnp.arange(BLOCK).astype(jnp.float32)
    spread = offsets[:, None] - offsets[None, :]
    causal = spread >= 0
    within = jnp.where(
        causal[None], jnp.exp(-rates[:, None, None] * jnp.where(causal, spread, 0.0)[None]), 0.0
    )
    first_decay = jnp.exp(-rates[:, None] * (offsets[None, :] + 1.0))
    last_decay = jnp.exp(-rates[:, None] * (BLOCK - 1.0 - offsets[None, :]))
    block_decay = jnp.exp(-rates * BLOCK)
    return (within, first_decay, last_decay, block_decay)


def to_blocks(values, heads):
    shaped = values.reshape(SEQ_DEV, SLOT // BLOCK, BLOCK, heads, HD)
    return shaped.transpose(1, 0, 3, 2, 4)


def from_blocks(blocks):
    return blocks.transpose(1, 0, 3, 2, 4).reshape(-1, blocks.shape[2] * blocks.shape[4])


def lightning_forward(query, keys, values, tables):
    within, first_decay, last_decay, block_decay = tables

    def advance(carried, inputs):
        query_blk, keys_blk, values_blk = inputs
        scores = jnp.einsum(
            "shbd,shcd->shbc", query_blk, keys_blk, preferred_element_type=jnp.float32
        )
        weights = (scores * within[None]).astype(jnp.bfloat16)
        inner_sum = jnp.einsum(
            "shbc,shcd->shbd", weights, values_blk, preferred_element_type=jnp.float32
        )
        outer_sum = first_decay[None, :, :, None] * exact(
            "shbd,shde->shbe", query_blk.astype(jnp.float32), carried
        )
        keys_scaled = keys_blk.astype(jnp.float32) * last_decay[None, :, :, None]
        update = exact("shbd,shbe->shde", keys_scaled, values_blk.astype(jnp.float32))
        return (
            block_decay[None, :, None, None] * carried + update,
            (inner_sum + outer_sum, carried),
        )

    initial = jnp.zeros((SEQ_DEV, query.shape[2], HD, HD), jnp.float32)
    final_state, (mixed, states) = lax.scan(advance, initial, (query, keys, values))
    return (mixed, states)


def lightning_backward(query, keys, values, grads, states, tables):
    within, first_decay, last_decay, block_decay = tables

    def retreat(later_grad, inputs):
        query_blk, keys_blk, values_blk, grad_blk, carried = inputs
        scores = jnp.einsum(
            "shbd,shcd->shbc", query_blk, keys_blk, preferred_element_type=jnp.float32
        )
        weights = (scores * within[None]).astype(jnp.bfloat16)
        d_weights = jnp.einsum(
            "shbd,shcd->shbc", grad_blk, values_blk, preferred_element_type=jnp.float32
        )
        d_scores = (d_weights * within[None]).astype(jnp.bfloat16)
        d_query = jnp.einsum(
            "shbc,shcd->shbd", d_scores, keys_blk, preferred_element_type=jnp.float32
        )
        d_keys = jnp.einsum(
            "shbc,shbd->shcd", d_scores, query_blk, preferred_element_type=jnp.float32
        )
        d_values = jnp.einsum(
            "shbc,shbd->shcd", weights, grad_blk, preferred_element_type=jnp.float32
        )
        grad_scaled = grad_blk.astype(jnp.float32) * first_decay[None, :, :, None]
        keys_scaled = keys_blk.astype(jnp.float32) * last_decay[None, :, :, None]
        d_query = d_query + exact("shbe,shde->shbd", grad_scaled, carried)
        d_keys = d_keys + last_decay[None, :, :, None] * exact(
            "shbe,shde->shbd", values_blk.astype(jnp.float32), later_grad
        )
        d_values = d_values + exact("shbd,shde->shbe", keys_scaled, later_grad)
        earlier = block_decay[None, :, None, None] * later_grad + exact(
            "shbd,shbe->shde", query_blk.astype(jnp.float32), grad_scaled
        )
        return (earlier, (d_query, d_keys, d_values))

    initial = jnp.zeros((SEQ_DEV, query.shape[2], HD, HD), jnp.float32)
    first_grad, results = lax.scan(
        retreat, initial, (query, keys, values, grads, states), reverse=True
    )
    return results


def body(
    tokens,
    lengths,
    decay,
    w_query,
    w_key,
    w_value,
    w_gate,
    w_out,
    f_value,
    f_gate,
    f_out,
    cotangent,
):
    own_rows = tokens.shape[0]
    first_row = lax.axis_index("head") * own_rows
    heads_here = decay.shape[0]
    tables = decay_tables(decay)
    positions = first_row + jnp.arange(own_rows, dtype=jnp.int32)
    slot_match = (positions // SLOT)[:, None] == jnp.arange(SEQ_DEV, dtype=jnp.int32)[None, :]
    length_of = jnp.sum(jnp.where(slot_match, lengths[None, :], 0), axis=1)
    keep_rows = (positions % SLOT < length_of).astype(jnp.float32)[:, None]
    inputs_f = tokens.astype(jnp.float32)
    normed, scale_in = normalize(inputs_f)
    gathered = lax.all_gather(normed.astype(jnp.bfloat16), "head", axis=0, tiled=True)
    query_pre = matmul(gathered, w_query)
    keys_pre = matmul(gathered, w_key)
    values_pre = matmul(gathered, w_value)
    gate_pre = matmul(gathered, w_gate)
    query_blocks = to_blocks(jax.nn.silu(query_pre).astype(jnp.bfloat16), heads_here)
    keys_blocks = to_blocks(jax.nn.silu(keys_pre).astype(jnp.bfloat16), heads_here)
    values_blocks = to_blocks(values_pre.astype(jnp.bfloat16), heads_here)
    mixed_blocks, states = lightning_forward(query_blocks, keys_blocks, values_blocks, tables)
    mixed = from_blocks(mixed_blocks)
    squares = lax.psum(jnp.sum(mixed * mixed, axis=1), "head")
    scale_out = lax.rsqrt(squares / D + epsilon)[:, None]
    mixed_unit = mixed * scale_out
    gated = (mixed_unit * gate_pre).astype(jnp.bfloat16)
    branch = lax.psum_scatter(
        matmul(gated, w_out).astype(jnp.bfloat16), "head", scatter_dimension=0, tiled=True
    ).astype(jnp.float32)
    middle = inputs_f + branch
    mid_normed, scale_mid = normalize(middle)
    mid_all = lax.all_gather(mid_normed.astype(jnp.bfloat16), "head", axis=0, tiled=True)
    value_full, gate_full = (
        lax.all_gather(f_value, "dp", axis=0, tiled=True),
        lax.all_gather(f_gate, "dp", axis=0, tiled=True),
    )
    down_full = lax.all_gather(f_out, "dp", axis=1, tiled=True)
    value_ffn = matmul(mid_all, value_full)
    gate_ffn = matmul(mid_all, gate_full)
    hidden = (value_ffn * gate_ffn).astype(jnp.bfloat16)
    ffn_branch = lax.psum_scatter(
        matmul(hidden, down_full).astype(jnp.bfloat16), "head", scatter_dimension=0, tiled=True
    ).astype(jnp.float32)
    output = ((middle + ffn_branch) * keep_rows).astype(jnp.bfloat16)
    grad_out = cotangent.astype(jnp.float32) * keep_rows
    grad_all = lax.all_gather(grad_out.astype(jnp.bfloat16), "head", axis=0, tiled=True)
    grad_hidden = matmul_right_t(grad_all, down_full)
    d_value_ffn = (grad_hidden * gate_ffn).astype(jnp.bfloat16)
    d_gate_ffn = (grad_hidden * value_ffn).astype(jnp.bfloat16)
    d_mid_normed = lax.psum_scatter(
        (matmul_right_t(d_value_ffn, value_full) + matmul_right_t(d_gate_ffn, gate_full)).astype(
            jnp.bfloat16
        ),
        "head",
        scatter_dimension=0,
        tiled=True,
    ).astype(jnp.float32)
    grad_middle = grad_out + norm_back(d_mid_normed, mid_normed, scale_mid)
    joined = jnp.concatenate([d_value_ffn, d_gate_ffn], axis=1)
    hidden_here = hidden.shape[1]
    shares = lax.psum_scatter(
        jnp.concatenate(
            [matmul_left_t(mid_all, joined), matmul_left_t(grad_all, hidden)], axis=1
        ).astype(jnp.bfloat16),
        "dp",
        scatter_dimension=0,
        tiled=True,
    ).astype(jnp.float32)
    d_f_value = shares[:, :hidden_here]
    d_f_gate = shares[:, hidden_here : 2 * hidden_here]
    d_f_out = shares[:, 2 * hidden_here :].T
    grad_rows = lax.all_gather(grad_middle.astype(jnp.bfloat16), "head", axis=0, tiled=True)
    d_gated = matmul_right_t(grad_rows, w_out)
    d_w_out_local = matmul_left_t(gated, grad_rows)
    d_gate_pre = (d_gated * mixed_unit).astype(jnp.bfloat16)
    d_unit = d_gated * gate_pre
    inner_out = lax.psum(jnp.sum(d_unit * mixed_unit, axis=1), "head")
    d_mixed = (scale_out * (d_unit - mixed_unit * (inner_out / D)[:, None])).astype(jnp.bfloat16)
    d_query, d_keys, d_values = lightning_backward(
        query_blocks, keys_blocks, values_blocks, to_blocks(d_mixed, heads_here), states, tables
    )
    d_query_pre = (from_blocks(d_query) * silu_slope(query_pre)).astype(jnp.bfloat16)
    d_keys_pre = (from_blocks(d_keys) * silu_slope(keys_pre)).astype(jnp.bfloat16)
    d_values_pre = from_blocks(d_values).astype(jnp.bfloat16)
    total = matmul_right_t(d_query_pre, w_query) + matmul_right_t(d_keys_pre, w_key)
    d_normed = lax.psum_scatter(
        (total + matmul_right_t(d_values_pre, w_value) + matmul_right_t(d_gate_pre, w_gate)).astype(
            jnp.bfloat16
        ),
        "head",
        scatter_dimension=0,
        tiled=True,
    ).astype(jnp.float32)
    d_tokens = grad_middle + norm_back(d_normed, normed, scale_in)
    grads_attention = (
        lax.psum(matmul_left_t(gathered, d_query_pre).astype(jnp.bfloat16), "dp").astype(
            jnp.float32
        ),
        lax.psum(matmul_left_t(gathered, d_keys_pre).astype(jnp.bfloat16), "dp").astype(
            jnp.float32
        ),
        lax.psum(matmul_left_t(gathered, d_values_pre).astype(jnp.bfloat16), "dp").astype(
            jnp.float32
        ),
        lax.psum(matmul_left_t(gathered, d_gate_pre).astype(jnp.bfloat16), "dp").astype(
            jnp.float32
        ),
        lax.psum(d_w_out_local.astype(jnp.bfloat16), "dp").astype(jnp.float32),
    )
    return (
        output,
        d_tokens,
        grads_attention[0],
        grads_attention[1],
        grads_attention[2],
        grads_attention[3],
        grads_attention[4],
        d_f_value,
        d_f_gate,
        d_f_out,
    )


def solution(mesh):
    placed = (
        P(("dp", "head"), None),
        P("dp"),
        P("head"),
        P(None, "head"),
        P(None, "head"),
        P(None, "head"),
        P(None, "head"),
        P("head", None),
        P("dp", "head"),
        P("dp", "head"),
        P("head", "dp"),
        P(("dp", "head"), None),
    )
    return jax.shard_map(
        body,
        mesh=mesh,
        in_specs=placed,
        out_specs=(
            P(("dp", "head"), None),
            P(("dp", "head"), None),
            P(None, "head"),
            P(None, "head"),
            P(None, "head"),
            P(None, "head"),
            P("head", None),
            P("dp", "head"),
            P("dp", "head"),
            P("head", "dp"),
        ),
        check_vma=False,
    )
```

profile of v0, /device:TPU:0, one launch (start us, length us, event | category | flops | bytes accessed | tf_op | source)
XLA Modules:
  0.0 686.0 jit_solution(16797415050043910649)
XLA Ops:
  15.0 33.8 %all-gather.8.cloned.1.call-done = bf16[1024,1024]{1,0:T(8,128)(2,1)} async-done(((bf16[512,1024]{1,0:T(8,128)(2,1)}), bf16[1024,1024]{1,0:T(8,128)(2,1)}) %all-gather.8.cloned.1.call-update) | async-done | bytes 2097168 | tf_op jit(solution)/shard_map/all_gather | solution.py:163
  69.1 15.1 %while.40 = (s32[]{:T(128)}, f32[1,4,128,128]{3,2,1,0:T(8,128)S(1)}, f32[2,1,4,512,128]{4,3,2,1,0:T(8,128)}, f32[2,1,4,128,128]{4,3,2,1,0:T(8,128)}, f32[4]{0:T(...) while((s32[]{:T(128)}, ...), condition=%wide.region_2.3_spmd.clone.clone.clone, body=%wide.region_1.2_spmd.clone.clone.clone.sunk | while | flops 1347751936 | bytes 17343232 | solution.py:94
  92.6 5.1 psum.49
  97.7 4.5 multiply_convert_fusion.6
  106.5 31.3 %reduce-scatter.6.cloned.1.call-done = bf16[512,1024]{1,0:T(8,128)(2,1)} async-done(((bf16[1024,1024]{1,0:T(8,128)(2,1)}), bf16[512,1024]{1,0:T(8,128)(2,1)}) %reduce-scatter.6.cloned.1.call-update) | async-done | bytes 1048592 | tf_op jit(solution)/shard_map/reduce_scatter | solution.py:177
  145.4 7.4 %all-gather.12.cloned.1.call-done = bf16[1024,1408]{1,0:T(8,128)(2,1)} async-done(((bf16[64,1408]{1,0:T(8,128)(2,1)}), bf16[1024,1408]{1,0:T(8,128)(2,1)}) %all-gather.12.cloned.1.call-update) | async-done | bytes 2883600 | tf_op jit(solution)/shard_map/all_gather | solution.py:184
  152.9 33.7 %all-gather.10.cloned.1.call-done = bf16[1024,1024]{1,0:T(8,128)(2,1)} async-done(((bf16[512,1024]{1,0:T(8,128)(2,1)}), bf16[1024,1024]{1,0:T(8,128)(2,1)}) %all-gather.10.cloned.1.call-update) | async-done | bytes 2097168 | tf_op jit(solution)/shard_map/all_gather | solution.py:182
  186.6 8.3 %fusion.155 = f32[1024,1408]{1,0:T(8,128)} fusion(bf16[1024,1024]{1,0:T(8,128)(2,1)} %all-gather.10.cloned.1.call-done, bf16[1024,1408]{1,0:T(8,128)(2,1)} %all-gather.12.cloned.1.call-done), kind=kOutput, calls=%fused_computation.209 | convolution fusion | flops 2952790016 | bytes 10747904 | tf_op jit(solution)/shard_map/dot_general | solution.py:30
  194.9 38.1 %all-gather.14.cloned.1.call-done = bf16[1024,1408]{1,0:T(8,128)(2,1)} async-done(((bf16[64,1408]{1,0:T(8,128)(2,1)}), bf16[1024,1408]{1,0:T(8,128)(2,1)}) %all-gather.14.cloned.1.call-update) | async-done | bytes 2883600 | tf_op jit(solution)/shard_map/all_gather | solution.py:185
  233.0 8.4 %fusion.156 = f32[1024,1408]{1,0:T(8,128)} fusion(bf16[1024,1024]{1,0:T(8,128)(2,1)} %all-gather.10.cloned.1.call-done, bf16[1024,1408]{1,0:T(8,128)(2,1)} %all-gather.14.cloned.1.call-done), kind=kOutput, calls=%fused_computation.210 | convolution fusion | flops 2952790016 | bytes 10747904 | tf_op jit(solution)/shard_map/dot_general | solution.py:30
  241.4 25.5 %all-gather.18.cloned.1.call-done = bf16[1024,1024]{1,0:T(8,128)(2,1)} async-done(((bf16[512,1024]{1,0:T(8,128)(2,1)}), bf16[1024,1024]{1,0:T(8,128)(2,1)}) %all-gather.18.cloned.1.call-update) | async-done | bytes 2097168 | tf_op jit(solution)/shard_map/all_gather | solution.py:196
  266.8 46.6 %all-gather.16.cloned.1.call-done = bf16[1408,1024]{0,1:T(8,128)(2,1)} async-done(((bf16[1408,64]{0,1:T(8,128)(2,1)}), bf16[1408,1024]{0,1:T(8,128)(2,1)}) %all-gather.16.cloned.1.call-update) | async-done | bytes 2883600 | tf_op jit(solution)/shard_map/all_gather | solution.py:187
  313.4 11.0 %multiply_convert_fusion = (bf16[1024,1408]{1,0:T(8,128)(2,1)S(1)}, bf16[1024,1408]{1,0:T(8,128)(2,1)}, bf16[1024,1408]{1,0:T(8,128)(2,1)S(1)}) fusion(f32[1024,1408]{1,0:T(8,128)} %fusion.155, f32[1024,1408]{1,0:T(8,128)} %fusion.156, bf16[1024,1024]{1,0:T(8,128)(2,1)} %all-gather.18.cloned.1.call-done, bf16[1408,1024]{0,1:T(8,128)(2,1)} %all-gather.16.cloned.1.call-done), kind=kOutput, calls=%fused_computation.120 | convolution fusion | flops 2961440768 | bytes 25165824 | tf_op jit(solution)/shard_map/dot_general | solution.py:34
  328.3 4.6 add_convert_fusion.1
  333.0 30.6 %reduce-scatter.10.cloned.1.call-done = bf16[512,1024]{1,0:T(8,128)(2,1)} async-done(((bf16[1024,1024]{1,0:T(8,128)(2,1)}), bf16[512,1024]{1,0:T(8,128)(2,1)}) %reduce-scatter.10.cloned.1.call-update) | async-done | bytes 1048592 | tf_op jit(solution)/shard_map/reduce_scatter | solution.py:200
  371.5 29.3 %all-gather.20.cloned.1.call-done = bf16[1024,1024]{1,0:T(8,128)(2,1)} async-done(((bf16[512,1024]{1,0:T(8,128)(2,1)}), bf16[1024,1024]{1,0:T(8,128)(2,1)}) %all-gather.20.cloned.1.call-update) | async-done | bytes 2097168 | tf_op jit(solution)/shard_map/all_gather | solution.py:222
  400.8 5.3 multiply_reduce_fusion
  406.1 4.9 psum.50
  418.9 36.7 %while.41 = (s32[]{:T(128)}, f32[1,4,128,128]{3,2,1,0:T(8,128)S(1)}, f32[2,1,4,512,128]{4,3,2,1,0:T(8,128)}, f32[2,1,4,512,128]{4,3,2,1,0:T(8,128)}, bf16[2,1,4,...) while((s32[]{:T(128)}, ...), condition=%wide.region_13.14_spmd.clone.clone.clone, body=%wide.region_12.13_spmd.clone.clone.clone.sunk | while | flops 2964131840 | bytes 44889964 | solution.py:133
  486.5 7.5 %convolution_convert_fusion.1 = bf16[1024,1024]{1,0:T(8,128)(2,1)} fusion(bf16[1024,1408]{1,0:T(8,128)(2,1)} %get-tuple-element.714, bf16[1408,1024]{0,1:T(8,128)(2,1)} %all-gather.16.cloned.1.call-done), kind=kOutput, calls=%fused_computation.160 | convolution fusion | flops 2953838592 | bytes 7864320 | tf_op jit(solution)/shard_map/dot_general | solution.py:30
  495.7 5.7 convolution_convert_fusion
  501.4 6.8 fusion.121
  512.1 115.8 %all-reduce.3.cloned.1.call-done = (bf16[1024,512]{1,0:T(8,128)(2,1)}, bf16[1024,512]{1,0:T(8,128)(2,1)}, bf16[1024,512]{1,0:T(8,128)(2,1)}, bf16[1024,512]{1,0:T(8,128)(2,1)}, bf16[512,1024]{1,0:T(8,128)(2,1)}) async-done(((bf16[1024,512]{1,0:T(8,128)(2,1)}, bf16[1024,512]{1,0:T(8,128)(2,1)}, bf16[1024,512]{1,0:T(8,128)(2,1)}, bf16[1024,512]{1,0:T(8,128)(2,1)}, bf16[512,1024]{1,0:T(8,128)(2,1)}), ...) | async-done | bytes 5242896 | tf_op jit(solution)/shard_map/psum | solution.py:246
  643.4 31.9 %reduce-scatter.14.cloned.1.call-done = bf16[64,4224]{1,0:T(8,128)(2,1)} async-done(((bf16[1024,4224]{1,0:T(8,128)(2,1)}), bf16[64,4224]{1,0:T(8,128)(2,1)}) %reduce-scatter.14.cloned.1.call-update) | async-done | bytes 540688 | tf_op jit(solution)/shard_map/reduce_scatter | solution.py:211
  (246 shorter events, 172.2 us)
Async XLA Ops:
  8.0 95.2 %copy-start = (bf16[512,1024]{1,0:T(8,128)(2,1)S(1)}, bf16[512,1024]{1,0:T(8,128)(2,1)}, u32[]{:S(2)}) copy-start(bf16[512,1024]{1,0:T(8,128)(2,1)} %param.23) | copy-start | bytes 3145732
  8.0 40.8 %all-gather.8.cloned.1.call-start = ((), (), s32[]{:S(2)}) async-start(), calls=%async_computation.5 | async-start | bytes 3145728 | tf_op jit(solution)/shard_map/all_gather | solution.py:163
  10.3 38.5 %copy-start.48 = (bf16[1024,512]{1,0:T(8,128)(2,1)S(1)}, bf16[1024,512]{1,0:T(8,128)(2,1)}, u32[]{:S(2)}) copy-start(bf16[1024,512]{1,0:T(8,128)(2,1)} %param.20) | copy-start | bytes 3145732
  12.8 125.0 %reduce-scatter.6.cloned.1.call-start = ((), (), s32[]{:S(2)}) async-start(), calls=%async_computation.6 | async-start | bytes 3145728 | tf_op jit(solution)/shard_map/reduce_scatter | solution.py:177
  84.2 6.3 copy-start.6
  92.5 9.6 %copy-start.4 = (f32[64,8,2,512]{3,1,2,0:T(8,128)}, f32[64,8,2,512]{3,1,2,0:T(8,128)S(1)}, u32[]{:S(2)}) copy-start(f32[64,8,2,512]{3,1,2,0:T(8,128)S(1)} %copy.52) | copy-start | bytes 6291460
  105.8 32.0 %copy-start.2 = (bf16[512,1024]{1,0:T(8,128)(2,1)S(1)}, bf16[512,1024]{1,0:T(8,128)(2,1)}, u32[]{:S(2)}) copy-start(bf16[512,1024]{1,0:T(8,128)(2,1)} %param.16) | copy-start | bytes 3145732
  105.8 47.0 %all-gather.12.cloned.1.call-start = ((), (), s32[]{:S(2)}) async-start(), calls=%async_computation.8 | async-start | bytes 3063808 | tf_op jit(solution)/shard_map/all_gather | solution.py:184
  106.4 80.2 %all-gather.10.cloned.1.call-start = ((), (), s32[]{:S(2)}) async-start(), calls=%async_computation.7 | async-start | bytes 3145728 | tf_op jit(solution)/shard_map/all_gather | solution.py:182
  140.8 92.1 %all-gather.14.cloned.1.call-start = ((), (), s32[]{:S(2)}) async-start(), calls=%async_computation.9 | async-start | bytes 3063808 | tf_op jit(solution)/shard_map/all_gather | solution.py:185
  141.4 125.4 %all-gather.18.cloned.1.call-start = ((), (), s32[]{:S(2)}) async-start(), calls=%async_computation.12 | async-start | bytes 3145728 | tf_op jit(solution)/shard_map/all_gather | solution.py:196
  144.6 168.8 %all-gather.16.cloned.1.call-start = ((), (), s32[]{:S(2)}) async-start(), calls=%async_computation.10 | async-start | bytes 3063808 | tf_op jit(solution)/shard_map/all_gather | solution.py:187
  145.4 218.3 %reduce-scatter.10.cloned.1.call-start = ((), (), s32[]{:S(2)}) async-start(), calls=%async_computation.13 | async-start | bytes 3145728 | tf_op jit(solution)/shard_map/reduce_scatter | solution.py:200
  313.4 11.0 %copy-start.44 = (bf16[1024,1408]{1,0:T(8,128)(2,1)S(1)}, bf16[1024,1408]{1,0:T(8,128)(2,1)}, u32[]{:S(2)}) copy-start(bf16[1024,1408]{1,0:T(8,128)(2,1)} %all-gather.12.cloned.1.call-done) | copy-start | bytes 8650756
  333.0 67.8 %all-gather.20.cloned.1.call-start = ((), (), s32[]{:S(2)}) async-start(), calls=%async_computation.14 | async-start | bytes 3145728 | tf_op jit(solution)/shard_map/all_gather | solution.py:222
  367.5 33.3 %copy-start.5 = (f32[64,8,2,512]{3,1,2,0:T(8,128)S(1)}, f32[64,8,2,512]{3,1,2,0:T(8,128)}, u32[]{:S(2)}) copy-start(f32[64,8,2,512]{3,1,2,0:T(8,128)} %copy-done.4) | copy-start | bytes 6291460
  367.5 260.3 %all-reduce.3.cloned.1.call-start = ((), (), s32[]{:S(2)}) async-start(), calls=%async_computation.17 | async-start | bytes 10485760 | tf_op jit(solution)/shard_map/psum | solution.py:246
  462.4 11.0 %copy-start.38 = (bf16[1,2,512,4,128]{4,3,2,1,0:T(4,128)(2,1)}, bf16[1,2,512,4,128]{4,3,2,1,0:T(4,128)(2,1)S(1)}, u32[]{:S(2)}) copy-start(bf16[1,2,512,4,128]{4,3,2,1,0:T(4,128)(2,1)S(1)} %copy.46) | copy-start | bytes 3145732
  478.0 159.2 %reduce-scatter.12.cloned.1.call-start = ((), (), s32[]{:S(2)}) async-start(), calls=%async_computation.15 | async-start | bytes 3145728 | tf_op jit(solution)/shard_map/reduce_scatter | solution.py:236
  486.5 152.5 %reduce-scatter.8.cloned.1.call-start = ((), (), s32[]{:S(2)}) async-start(), calls=%async_computation.11 | async-start | bytes 3145728 | tf_op jit(solution)/shard_map/reduce_scatter | solution.py:191
  494.1 181.3 %reduce-scatter.14.cloned.1.call-start = ((), (), s32[]{:S(2)}) async-start(), calls=%async_computation.16 | async-start | bytes 9191424 | tf_op jit(solution)/shard_map/reduce_scatter | solution.py:211
  495.7 5.7 copy-start.28
  495.7 5.7 copy-start.46
  639.0 39.3 %copy-start.1 = (bf16[512,1024]{1,0:T(8,128)(2,1)S(1)}, bf16[512,1024]{1,0:T(8,128)(2,1)}, u32[]{:S(2)}) copy-start(bf16[512,1024]{1,0:T(8,128)(2,1)} %param.23) | copy-start | bytes 3145732
  (49 other events, 118.3 us)
Sparse Core Ops, SparseCore 0:
  12.9 35.8 all-gather.7
  106.0 31.7 reduce-scatter.5
  333.1 30.4 reduce-scatter.9
  367.6 33.1 all-gather.19
  486.6 31.8 reduce-scatter.11
  520.7 31.8 reduce-scatter.7
  557.2 118.1 reduce-scatter.13
Sparse Core Ops, SparseCore 1:
  108.9 43.9 all-gather.11
  154.9 31.6 all-gather.9
  189.0 43.9 all-gather.13
  235.2 31.6 all-gather.17
  269.4 43.9 all-gather.15
  478.1 149.7 all-reduce.2
where the time goes:
time: 694 us; the launch traced here: 686 us
  waiting for transfers between devices  426 us (61%)
  matrix products  147 us (21%)
  other arithmetic  43.4 us (6%)
  local copies, waits for them, and re-layouts  41 us (6%)
  between operations  17.1 us (2%)
  blocking collectives  10 us (1%)
    psum x1, waiting for transfers between devices, body(): lax.psum(matmul_left_t(gathered, d_query_pre).astype(jnp.bfloat16), 'dp')  116 us
    all_gather x1, waiting for transfers between devices, body(): down_full = lax.all_gather(f_out, 'dp', axis=1, tiled=True)  46.6 us
    dot_general x8, matrix products, matmul(): return jnp.dot(left_side, right_side, preferred_element_type=jnp.float32)  41.9 us
    all_gather x1, waiting for transfers between devices, body(): lax.all_gather(f_gate, 'dp', axis=0, tiled=True)  38.1 us
    all_gather x1, waiting for transfers between devices, body(): lax.all_gather(normed.astype(jnp.bfloat16), 'head', axis=0, tiled=True)  33.8 us
    all_gather x1, waiting for transfers between devices, body(): lax.all_gather(mid_normed.astype(jnp.bfloat16), 'head', axis=0, tiled=True)  33.7 us
    dot_general x8, matrix products, matmul_right_t(): lax.dot_general(left_side, right_side, (((1,), (1,)), ((), ())), preferre...  32.3 us
    reduce_scatter x1, waiting for transfers between devices, body(): lax.psum_scatter(jnp.concatenate([matmul_left_t(mid_all, joined), matmul_...  31.9 us
  transfers between devices with their start and end apart: 13, of which 11 were waited for; matrix products, arithmetic and copies ran while one was open for 11% of the time, Pallas kernels for 0%

commit v1 on v0

--- a/solution.py
+++ b/solution.py
@@ -1,7 +1,9 @@
+import functools
 import jax
 import jax.numpy as jnp
 from jax import lax
 from jax.sharding import PartitionSpec as P
+from jax.lax import axis_index, axis_size, ppermute
 
 D = 1024
 HD = 128
@@ -9,6 +11,25 @@
 SLOT = 1024
 BLOCK = 512
 epsilon = 1e-06
+
+
+def part_kinds_up(block_in, row_axis):
+    axis_total = axis_size(row_axis)
+    crops = list(map(lambda d: (d, (d + 1) % axis_total), range(axis_total)))
+    fields = list(map(lambda d: (d, (d - 1) % axis_total), range(axis_total)))
+    extra, small = ([block_in], [block_in])
+    for _ in range(axis_total // 2):
+        extra.append(ppermute(extra[-1], row_axis, crops))
+    for _ in tuple(range((axis_total - 1) // 2)):
+        small.append(ppermute(small[-1], row_axis, fields))
+    part_now = jnp.concatenate([*extra[::-1], *small[1:]], 0)
+    f_next = jnp.roll(
+        part_now, shift=(axis_index(row_axis) - axis_total // 2) * block_in.shape[0], axis=0
+    )
+    return f_next
+
+
+meshes_pass = functools.partial(part_kinds_up, row_axis="dp")
 
 
 def normalize(values):
@@ -180,10 +201,7 @@
     middle = inputs_f + branch
     mid_normed, scale_mid = normalize(middle)
     mid_all = lax.all_gather(mid_normed.astype(jnp.bfloat16), "head", axis=0, tiled=True)
-    value_full, gate_full = (
-        lax.all_gather(f_value, "dp", axis=0, tiled=True),
-        lax.all_gather(f_gate, "dp", axis=0, tiled=True),
-    )
+    value_full, gate_full = (lax.all_gather(f_value, "dp", axis=0, tiled=True), meshes_pass(f_gate))
     down_full = lax.all_gather(f_out, "dp", axis=1, tiled=True)
     value_ffn = matmul(mid_all, value_full)
     gate_ffn = matmul(mid_all, gate_full)

time: 694 us -> 797 us (1.15)
  waiting for transfers between devices: 426 us -> 469 us
  starting transfers between devices: 1.41 us -> 33 us
  local copies, waits for them, and re-layouts: 41 us -> 71.2 us
    reduce_scatter x1, waiting for transfers between devices: 31.9 us -> 107 us  [body(): lax.psum_scatter(jnp.concatenate([matmul_left_t(mid_all, joined), matmul_...]
    all_gather x1 -> x0, waiting for transfers between devices: 38.1 us -> none  [body(): lax.all_gather(f_gate, 'dp', axis=0, tiled=True)]
    all_gather x1, waiting for transfers between devices: 46.6 us -> 14 us  [body(): down_full = lax.all_gather(f_out, 'dp', axis=1, tiled=True)]
    reduce_scatter x1, waiting for transfers between devices: 0.02 us -> 32.4 us  [body(): lax.psum_scatter(matmul(hidden, down_full).astype(jnp.bfloat16), 'head',...]
    reduce_scatter x1, waiting for transfers between devices: 31.3 us -> 0.01 us  [body(): lax.psum_scatter(matmul(gated, w_out).astype(jnp.bfloat16), 'head', scatt...]
    ppermute x0 -> x15, starting transfers between devices: none -> 31.3 us  [the longest x7 31.2 us: part_kinds_up(): small.append(ppermute(small[-1], row_axis, fields))]
    ppermute x0 -> x15, waiting for transfers between devices: none -> 30.6 us  [the longest x8 30.5 us: part_kinds_up(): extra.append(ppermute(extra[-1], row_axis, crops))]
    all_gather x1, waiting for transfers between devices: 7.44 us -> 36.7 us  [body(): lax.all_gather(f_value, 'dp', axis=0, tiled=True)]
  transfers between devices with their start and end apart: 13 -> 27, of which waited for: 11 -> 18; matrix products, arithmetic and copies ran while one was open for 11% -> 12% of each run, Pallas kernels for 0% -> 0%
where the time goes in v1:
time: 797 us; the launch traced here: 789 us
  waiting for transfers between devices  469 us (59%)
  matrix products  147 us (18%)
  local copies, waits for them, and re-layouts  71.2 us (9%)
  other arithmetic  42.1 us (5%)
  starting transfers between devices  33 us (4%)
  between operations  15.7 us (2%)
  blocking collectives  10.1 us (1%)
    reduce_scatter x1, waiting for transfers between devices, body(): lax.psum_scatter(jnp.concatenate([matmul_left_t(mid_all, joined), matmul_...  107 us
    psum x1, waiting for transfers between devices, body(): lax.psum(matmul_left_t(gathered, d_query_pre).astype(jnp.bfloat16), 'dp')  93 us
    dot_general x8, matrix products, matmul(): return jnp.dot(left_side, right_side, preferred_element_type=jnp.float32)  39.1 us
    unnamed x141, local copies, waits for them, and re-layouts  36.9 us
    all_gather x1, waiting for transfers between devices, body(): lax.all_gather(f_value, 'dp', axis=0, tiled=True)  36.7 us
    dot_general x8, matrix products, matmul_right_t(): lax.dot_general(left_side, right_side, (((1,), (1,)), ((), ())), preferre...  35.5 us
    all_gather x1, waiting for transfers between devices, body(): lax.all_gather(normed.astype(jnp.bfloat16), 'head', axis=0, tiled=True)  33.8 us
    all_gather x1, waiting for transfers between devices, body(): lax.all_gather(mid_normed.astype(jnp.bfloat16), 'head', axis=0, tiled=True)  33.5 us
  transfers between devices with their start and end apart: 27, of which 18 were waited for; matrix products, arithmetic and copies ran while one was open for 12% of the time, Pallas kernels for 0%

profile of v1, /device:TPU:0, one launch (start us, length us, event | category | flops | bytes accessed | tf_op | source)
XLA Modules:
  0.0 788.7 jit_solution(3718567665374630111)
XLA Ops:
  14.2 33.8 %all-gather.7.cloned.1.call-done = bf16[1024,1024]{1,0:T(8,128)(2,1)} async-done(((bf16[512,1024]{1,0:T(8,128)(2,1)}), bf16[1024,1024]{1,0:T(8,128)(2,1)}) %all-gather.7.cloned.1.call-update) | async-done | bytes 2097168 | tf_op jit(solution)/shard_map/all_gather | solution.py:184
  68.3 15.1 %while.40 = (s32[]{:T(128)}, f32[1,4,128,128]{3,2,1,0:T(8,128)S(1)}, f32[2,1,4,512,128]{4,3,2,1,0:T(8,128)}, f32[2,1,4,128,128]{4,3,2,1,0:T(8,128)}, f32[4]{0:T(...) while((s32[]{:T(128)}, ...), condition=%wide.region_2.3_spmd.clone.clone.clone, body=%wide.region_1.2_spmd.clone.clone.clone.sunk | while | flops 1347751936 | bytes 17343232 | solution.py:115
  91.7 5.2 psum.49
  108.3 7.6 collective-permute-done
  205.2 14.0 %all-gather.13.cloned.1.call-done = bf16[1408,1024]{0,1:T(8,128)(2,1)} async-done(((bf16[1408,64]{0,1:T(8,128)(2,1)}), bf16[1408,1024]{0,1:T(8,128)(2,1)}) %all-gather.13.cloned.1.call-update) | async-done | bytes 2883600 | tf_op jit(solution)/shard_map/all_gather | solution.py:205
  219.2 8.4 %fusion.164 = f32[1024,1408]{1,0:T(8,128)} fusion(bf16[1024,1024]{1,0:T(8,128)(2,1)} %all-gather.15.cloned.1.call-done, bf16[1408,1024]{0,1:T(8,128)(2,1)} %all-gather.13.cloned.1.call-done), kind=kOutput, calls=%fused_computation.248 | convolution fusion | flops 2952790016 | bytes 10747904 | tf_op jit(solution)/shard_map/dot_general | solution.py:55
  227.6 36.7 %all-gather.11.cloned.1.call-done = bf16[1024,1408]{1,0:T(8,128)(2,1)} async-done(((bf16[64,1408]{1,0:T(8,128)(2,1)}), bf16[1024,1408]{1,0:T(8,128)(2,1)}) %all-gather.11.cloned.1.call-update) | async-done | bytes 2883600 | tf_op jit(solution)/shard_map/all_gather | solution.py:204
  264.4 33.5 %all-gather.9.cloned.1.call-done = bf16[1024,1024]{1,0:T(8,128)(2,1)} async-done(((bf16[512,1024]{1,0:T(8,128)(2,1)}), bf16[1024,1024]{1,0:T(8,128)(2,1)}) %all-gather.9.cloned.1.call-update) | async-done | bytes 2097168 | tf_op jit(solution)/shard_map/all_gather | solution.py:203
  297.9 6.0 fusion.163
  303.9 7.8 multiply_convert_fusion
  311.8 7.3 fusion.165
  319.1 6.5 add_convert_fusion.1
  325.7 31.9 %reduce-scatter.10.cloned.1.call-done = bf16[512,1024]{1,0:T(8,128)(2,1)} async-done(((bf16[1024,1024]{1,0:T(8,128)(2,1)}), bf16[512,1024]{1,0:T(8,128)(2,1)}) %reduce-scatter.10.cloned.1.call-update) | async-done | bytes 1048592 | tf_op jit(solution)/shard_map/reduce_scatter | solution.py:218
  365.2 29.5 %all-gather.17.cloned.1.call-done = bf16[1024,1024]{1,0:T(8,128)(2,1)} async-done(((bf16[512,1024]{1,0:T(8,128)(2,1)}), bf16[1024,1024]{1,0:T(8,128)(2,1)}) %all-gather.17.cloned.1.call-update) | async-done | bytes 2097168 | tf_op jit(solution)/shard_map/all_gather | solution.py:240
  394.8 5.3 multiply_reduce_fusion
  400.1 4.9 psum.50
  412.9 36.7 %while.41 = (s32[]{:T(128)}, f32[1,4,128,128]{3,2,1,0:T(8,128)S(1)}, f32[2,1,4,512,128]{4,3,2,1,0:T(8,128)}, f32[2,1,4,512,128]{4,3,2,1,0:T(8,128)}, bf16[2,1,4,...) while((s32[]{:T(128)}, ...), condition=%wide.region_13.14_spmd.clone.clone.clone, body=%wide.region_12.13_spmd.clone.clone.clone.sunk | while | flops 2964131840 | bytes 44889964 | solution.py:154
  480.8 7.5 convolution_convert_fusion.1
  488.6 6.1 convolution_convert_fusion
  494.8 6.8 fusion.121
  505.4 93.0 %all-reduce.3.cloned.1.call-done = (bf16[1024,512]{1,0:T(8,128)(2,1)}, bf16[1024,512]{1,0:T(8,128)(2,1)}, bf16[1024,512]{1,0:T(8,128)(2,1)}, bf16[1024,512]{1,0:T(8,128)(2,1)}, bf16[512,1024]{1,0:T(8,128)(2,1)}) async-done(((bf16[1024,512]{1,0:T(8,128)(2,1)}, bf16[1024,512]{1,0:T(8,128)(2,1)}, bf16[1024,512]{1,0:T(8,128)(2,1)}, bf16[1024,512]{1,0:T(8,128)(2,1)}, bf16[512,1024]{1,0:T(8,128)(2,1)}), ...) | async-done | bytes 5242896 | tf_op jit(solution)/shard_map/psum | solution.py:264
  607.8 25.1 %reduce-scatter.12.cloned.1.call-done = bf16[512,1024]{1,0:T(8,128)(2,1)} async-done(((bf16[1024,1024]{1,0:T(8,128)(2,1)}), bf16[512,1024]{1,0:T(8,128)(2,1)}) %reduce-scatter.12.cloned.1.call-update) | async-done | bytes 1048592 | tf_op jit(solution)/shard_map/reduce_scatter | solution.py:254
  634.7 32.4 %reduce-scatter.8.cloned.1.call-done = bf16[512,1024]{1,0:T(8,128)(2,1)} async-done(((bf16[1024,1024]{1,0:T(8,128)(2,1)}), bf16[512,1024]{1,0:T(8,128)(2,1)}) %reduce-scatter.8.cloned.1.call-update) | async-done | bytes 1048592 | tf_op jit(solution)/shard_map/reduce_scatter | solution.py:209
  671.5 107.3 %reduce-scatter.14.cloned.1.call-done = bf16[64,4224]{1,0:T(8,128)(2,1)} async-done(((bf16[1024,4224]{1,0:T(8,128)(2,1)}), bf16[64,4224]{1,0:T(8,128)(2,1)}) %reduce-scatter.14.cloned.1.call-update) | async-done | bytes 540688 | tf_op jit(solution)/shard_map/reduce_scatter | solution.py:229
  (325 shorter events, 255.5 us)
Async XLA Ops:
  7.2 40.8 %all-gather.7.cloned.1.call-start = ((), (), s32[]{:S(2)}) async-start(), calls=%async_computation.5 | async-start | bytes 3145728 | tf_op jit(solution)/shard_map/all_gather | solution.py:184
  12.0 181.8 %reduce-scatter.6.cloned.1.call-start = ((), (), s32[]{:S(2)}) async-start(), calls=%async_computation.6 | async-start | bytes 3145728 | tf_op jit(solution)/shard_map/reduce_scatter | solution.py:198
  105.1 100.1 %all-gather.15.cloned.1.call-start = ((), (), s32[]{:S(2)}) async-start(), calls=%async_computation.11 | async-start | bytes 3145728 | tf_op jit(solution)/shard_map/all_gather | solution.py:214
  107.6 111.7 %all-gather.13.cloned.1.call-start = ((), (), s32[]{:S(2)}) async-start(), calls=%async_computation.9 | async-start | bytes 3063808 | tf_op jit(solution)/shard_map/all_gather | solution.py:205
  108.2 156.2 %all-gather.11.cloned.1.call-start = ((), (), s32[]{:S(2)}) async-start(), calls=%async_computation.8 | async-start | bytes 3063808 | tf_op jit(solution)/shard_map/all_gather | solution.py:204
  123.5 7.7 collective-permute-start.2
  123.5 7.7 collective-permute-start.9
  131.2 7.7 collective-permute-start.3
  131.3 7.7 collective-permute-start.10
  139.0 7.7 collective-permute-start.4
  139.0 7.7 collective-permute-start.11
  146.7 7.7 collective-permute-start.5
  146.7 7.7 collective-permute-start.12
  154.4 7.8 collective-permute-start.6
  154.4 7.9 %collective-permute-start.13 = (bf16[64,1408]{1,0:T(8,128)(2,1)S(1)}, bf16[64,1408]{1,0:T(8,128)(2,1)}, u32[]{:S(2)}, u32[]{:S(2)}) collective-permute-start(bf16[64,1408]{1,0:T(8,128)(2,1)S(1)} %collective-permute-done.12), channel_id=1, source_target_pairs={{0,30},{2,0},{4,2},{6,4},{8,6},{10,8},{12,10},{14,12},{16,14},{18,... | collective-permute-start | bytes 540680 | tf_op jit(solution)/shard_map/ppermute | solution.py:24
  162.3 7.9 %collective-permute-start.7 = (bf16[64,1408]{1,0:T(8,128)(2,1)}, bf16[64,1408]{1,0:T(8,128)(2,1)}, u32[]{:S(2)}, u32[]{:S(2)}) collective-permute-start(bf16[64,1408]{1,0:T(8,128)(2,1)} %collective-permute-done.6), channel_id=1, source_target_pairs={{0,2},{2,4},{4,6},{6,8},{8,10},{10,12},{12,14},{14,16},{16,18},{18... | collective-permute-start | bytes 540680 | tf_op jit(solution)/shard_map/ppermute | solution.py:22
  162.3 135.6 %all-gather.9.cloned.1.call-start = ((), (), s32[]{:S(2)}) async-start(), calls=%async_computation.7 | async-start | bytes 3145728 | tf_op jit(solution)/shard_map/all_gather | solution.py:203
  162.4 21.0 %collective-permute-start.14 = (bf16[64,1408]{1,0:T(8,128)(2,1)}, bf16[64,1408]{1,0:T(8,128)(2,1)S(1)}, u32[]{:S(2)}, u32[]{:S(2)}) collective-permute-start(bf16[64,1408]{1,0:T(8,128)(2,1)} %collective-permute-done.13), channel_id=1, source_target_pairs={{0,30},{2,0},{4,2},{6,4},{8,6},{10,8},{12,10},{14,12},{16,14},{18,... | collective-permute-start | bytes 540680 | tf_op jit(solution)/shard_map/ppermute | solution.py:24
  196.9 160.8 %reduce-scatter.10.cloned.1.call-start = ((), (), s32[]{:S(2)}) async-start(), calls=%async_computation.12 | async-start | bytes 3145728 | tf_op jit(solution)/shard_map/reduce_scatter | solution.py:218
  325.7 69.1 %all-gather.17.cloned.1.call-start = ((), (), s32[]{:S(2)}) async-start(), calls=%async_computation.13 | async-start | bytes 3145728 | tf_op jit(solution)/shard_map/all_gather | solution.py:240
  361.5 237.0 %all-reduce.3.cloned.1.call-start = ((), (), s32[]{:S(2)}) async-start(), calls=%async_computation.16 | async-start | bytes 10485760 | tf_op jit(solution)/shard_map/psum | solution.py:264
  472.0 160.9 %reduce-scatter.12.cloned.1.call-start = ((), (), s32[]{:S(2)}) async-start(), calls=%async_computation.14 | async-start | bytes 3145728 | tf_op jit(solution)/shard_map/reduce_scatter | solution.py:254
  480.8 186.3 %reduce-scatter.8.cloned.1.call-start = ((), (), s32[]{:S(2)}) async-start(), calls=%async_computation.10 | async-start | bytes 3145728 | tf_op jit(solution)/shard_map/reduce_scatter | solution.py:209
  488.4 290.4 %reduce-scatter.14.cloned.1.call-start = ((), (), s32[]{:S(2)}) async-start(), calls=%async_computation.15 | async-start | bytes 9191424 | tf_op jit(solution)/shard_map/reduce_scatter | solution.py:229
  (73 other events, 841.2 us)
Sparse Core Ops, SparseCore 0:
  12.1 35.8 all-gather.6
  105.3 31.8 reduce-scatter.5
  139.3 33.0 all-gather.14
  174.8 44.3 all-gather.12
  221.6 42.6 all-gather.10
  266.4 31.4 all-gather.8
  325.8 31.8 reduce-scatter.9
  361.6 33.1 all-gather.16
  472.1 126.2 all-reduce.2
  601.2 31.6 reduce-scatter.11
  635.2 31.8 reduce-scatter.7
  671.5 107.2 reduce-scatter.13
